TPU v7x, 256 devices: a whole 4x4x8 slice. The times are simulated.
256 devices in a mesh: gx: 8 (over y, core), gy: 4 (over z_lo), gz: 8 (over x, z_hi).
Axes of the slice: x: 4, y: 4, z: 8 (z_hi: 2, z_lo: 4; z = z_hi * 4 + z_lo), core: 2. Of those that a mesh axis runs over, the one named last changes fastest.
Arguments:
- wavefunctions: float32 [96, 48, 96, 256], P('gx', 'gy', 'gz'), may hold values from -6 to 6
- cell_matrices: bfloat16 [16, 8, 16, 343, 343], P('gx', 'gy', 'gz'), may hold values from -0.078125 to 0.078125
- projectors: float32 [256, 16, 1728], P(('gx', 'gy', 'gz')), may hold values from -0.14433756 to 0.14433756
- slot_atoms: int32 [256, 16], P(('gx', 'gy', 'gz')), may hold values from 0 to 512, as said below
- atom_coupling: float32 [512], replicated, may hold values from 0.5 to 3
Outputs:
- filtered: float32 [96, 48, 96, 256], P('gx', 'gy', 'gz')
Inputs may be any that keep to these rules, and one draw needn't show every extreme that they name: `slot_atoms`: atom a belongs to device a // 2. The live slots of device d name distinct atoms whose owners lie 0 or 1 below d along each of gx, gy, gz (periodically); 512 marks an empty slot, and some device has all 16 slots live.
All inputs are finite; a program needn't handle non-finite values.
Results may differ from a plain program's by a relative error of at most 0.00045.
Values may be sent and summed in bfloat16 or wider, within the bound.
A program may use at most 64 MiB of HBM per device.

v0:
```python
import itertools

import jax
import jax.numpy as jnp
from jax import lax
from jax.experimental import pallas as pl
from jax.experimental.pallas import tpu as pltpu
from jax.sharding import PartitionSpec as P

MESH = pl.DeviceIdType.MESH
F32 = jnp.float32
BF16 = jnp.bfloat16

LINES = 169
HALF = LINES * 8
ROWS = 2 * HALF
BLOCK = 104
PAD_NODES = 392

ALL = [d for d in itertools.product((-1, 0, 1), repeat=3) if any(d)]
ALL.sort(key=lambda d: sum(map(abs, d)))
DOWN = [d for d in ALL if max(d) <= 0]
UP = [d for d in ALL if min(d) >= 0]
BITS = [d for d in itertools.product((0, 1), repeat=3) if any(d)]


def kind_of(delta):
    return tuple(int(d != 0) for d in delta)


def message_rows(kind):
    return {
        (1, 0, 0): 208,
        (0, 1, 0): 208,
        (0, 0, 1): 169,
        (1, 1, 0): 16,
        (1, 0, 1): 13,
        (0, 1, 1): 13,
        (1, 1, 1): 1,
    }[kind]


def message_type(kind):
    return F32 if kind == (1, 1, 1) else BF16


def z_row(z):
    return 0 if z == 0 else HALF + 6


def pieces_of(kind, coords):
    x, y, z = coords
    if kind == (1, 0, 0):
        return [(k * HALF + x * BLOCK, BLOCK, 1) for k in (0, 1)]
    if kind == (0, 1, 0):
        return [(k * HALF + (13 * i + y) * 8, 8, 1) for k in (0, 1) for i in range(13)]
    if kind == (0, 0, 1):
        return [(z_row(z), LINES, 8)]
    if kind == (1, 1, 0):
        return [(k * HALF + (13 * x + y) * 8, 8, 1) for k in (0, 1)]
    if kind == (1, 0, 1):
        return [(z_row(z) + x * BLOCK, 13, 8)]
    if kind == (0, 1, 1):
        return [(z_row(z) + y * 8, 13, BLOCK)]
    return [(z_row(z) + (13 * x + y) * 8, 1, 1)]


def rows_at(start, count, stride):
    return pl.ds(start, count) if stride == 1 else pl.ds(start, count, stride)


def packed(field, h, kind, coords):
    parts = [field[h, rows_at(*p), :] for p in pieces_of(kind, coords)]
    return parts[0] if len(parts) == 1 else jnp.concatenate(parts, axis=0)


def merge(field, h, kind, coords, message, adding):
    at = 0
    for start, count, stride in pieces_of(kind, coords):
        part = message[at : at + count]
        rows = rows_at(start, count, stride)
        field[h, rows, :] = field[h, rows, :] + part if adding else part
        at += count


def both_halves(field, rows):
    return jnp.concatenate([field[0, rows, :], field[1, rows, :]], axis=1)


def neighbour(delta):
    out = []
    for name, d in zip(("gx", "gy", "gz"), delta):
        size = lax.axis_size(name)
        out.append((lax.axis_index(name) + d + size) % size)
    return tuple(out)


def start_exchange(field, deltas, send, recv, send_sem, recv_sem):
    copies = []
    for at, delta in enumerate(deltas):
        kind = kind_of(delta)
        coords = tuple(12 if d > 0 else 0 for d in delta)
        for h in (0, 1):
            send[at][h] = packed(field, h, kind, coords).astype(message_type(kind))
        copy = pltpu.make_async_remote_copy(
            src_ref=send[at],
            dst_ref=recv[at],
            send_sem=send_sem.at[at],
            recv_sem=recv_sem.at[at],
            device_id=neighbour(delta),
            device_id_type=MESH,
        )
        copy.start()
        copies.append(copy)
    return copies


def end_exchange(field, deltas, copies, recv, adding):
    for at, delta in enumerate(deltas):
        copies[at].wait_recv()
        coords = tuple(12 if d < 0 else 0 for d in delta)
        for h in (0, 1):
            merge(field, h, kind_of(delta), coords, recv[at][h].astype(F32), adding)


def exact_halves(values):
    high = values.astype(BF16)
    return high, (values - high.astype(F32)).astype(BF16)


def mm(a, b):
    return jnp.dot(a, b, preferred_element_type=F32)


def mm_nt(a, b):
    return lax.dot_general(a, b, (((1,), (1,)), ((), ())), preferred_element_type=F32)


def kernel(w_ref, k_ref, p_ref, slots_ref, coupling_ref, out_ref, *scratch):
    (field, image, pad_k, proj, proj_n, proj_t) = scratch[:6]
    nl_send, nl_recv, nl_own, nl_back, nl_sems = scratch[6:11]
    sems = scratch[11]
    buffers = scratch[12:]
    at = 0
    groups = []
    sem_at = 0
    for deltas in (DOWN, ALL, UP):
        n = len(deltas)
        groups.append(
            (
                buffers[at : at + n],
                buffers[at + n : at + 2 * n],
                sems.at[0, pl.ds(sem_at, n)],
                sems.at[1, pl.ds(sem_at, n)],
            )
        )
        at += 2 * n
        sem_at += n

    barrier = pltpu.get_barrier_semaphore()
    for delta in ALL:
        pl.semaphore_signal(barrier, inc=1, device_id=neighbour(delta), device_id_type=MESH)

    field[...] = jnp.zeros((2, ROWS, 128), F32)

    def spread(x, carry):
        low = w_ref[x, :, 0:8, :]
        high = w_ref[x, :, 8:12, :]
        high = jnp.concatenate([high, high], axis=1)
        row = lax.broadcasted_iota(jnp.int32, (12, 8, 256), 1)
        upper = jnp.where(row < 2, pltpu.roll(low, 2, 1), jnp.where(row < 6, pltpu.roll(high, 2, 1), 0.0))
        base = pl.multiple_of(x * BLOCK, 8)
        for h in (0, 1):
            lanes = slice(128 * h, 128 * h + 128)
            field[h, pl.ds(base, 96), :] = low[:, :, lanes].reshape(96, 128)
            field[h, pl.ds(base + HALF, 96), :] = upper[:, :, lanes].reshape(96, 128)
        return carry

    lax.fori_loop(0, 12, spread, 0)
    pl.semaphore_wait(barrier, len(ALL))
    all_copies = []
    first = start_exchange(field, DOWN, *groups[0])
    all_copies += first

    ids = slots_ref[...]
    owner = ids >> 1
    d_x = (lax.axis_index("gx") - (owner >> 5)) & 7
    d_y = (lax.axis_index("gy") - ((owner >> 3) & 3)) & 3
    d_z = (lax.axis_index("gz") - (owner & 7)) & 7
    place = ((d_x * 2 + d_y) * 2 + d_z) * 2 + (ids & 1)
    place = jnp.where(ids < coupling_ref.shape[0], place, -1)
    order = jnp.broadcast_to(place, (16, 16)) == lax.broadcasted_iota(jnp.int32, (16, 16), 0)
    order = jnp.where(order, 1.0, 0.0).astype(BF16)
    p_high, p_low = exact_halves(p_ref[...])
    proj[...] = jnp.zeros((48, 1920), BF16)
    p_high = mm(order, p_high).astype(BF16)
    p_low = mm(order, p_low).astype(BF16)
    proj[:, pl.ds(0, 1728)] = jnp.concatenate([p_high, p_low, p_high], axis=0)

    def spread_projectors(x, carry):
        begin = pl.multiple_of((x * 144) // 128 * 128, 128)
        window = proj[:, pl.ds(begin, 384)]
        row = lax.broadcasted_iota(jnp.int32, (2 * BLOCK, 1), 0)
        k = jnp.where(row >= BLOCK, 1, 0)
        inner = row - k * BLOCK
        y = inner >> 3
        r = inner & 7
        live = (y < 12) & (r < 7) & ((k == 0) | ((r >= 1) & (r <= 5)))
        target = jnp.where(live, 144 * x - begin + 12 * y + 6 * k + r, -1)
        pick = lax.broadcasted_iota(jnp.int32, (2 * BLOCK, 384), 1) == target
        pick = jnp.where(pick, 1.0, 0.0)
        for half in (0, 1):
            sel = pick[half * BLOCK : (half + 1) * BLOCK].astype(BF16)
            proj_t[half * 12 + x] = mm_nt(sel, window).astype(BF16)
            proj_n[half * 12 + x] = mm_nt(window[0:32], sel).astype(BF16)
        return carry

    lax.fori_loop(0, 12, spread_projectors, 0)

    def block_start(kx):
        return pl.multiple_of((kx // 12) * HALF + (kx % 12) * BLOCK, 8)

    def start_coefficients(values, app):
        def step(kx, total):
            high, low = exact_halves(both_halves(values, pl.ds(block_start(kx), BLOCK)))
            rows = proj_n[kx]
            both = mm(rows, high)
            return total + both[0:16] + both[16:32] + mm(rows[0:16], low)

        total = lax.fori_loop(0, 24, step, jnp.zeros((16, 256), F32))
        for g in range(8):
            nl_send[app, g] = total[2 * g : 2 * g + 2]
        copies = []
        for at, bits in enumerate(BITS):
            copy = pltpu.make_async_remote_copy(
                src_ref=nl_send.at[app, at + 1],
                dst_ref=nl_recv.at[app, at + 1],
                send_sem=nl_sems.at[0, app, at],
                recv_sem=nl_sems.at[1, app, at],
                device_id=neighbour(tuple(-b for b in bits)),
                device_id_type=MESH,
            )
            copy.start()
            copies.append(copy)
        return copies

    def start_totals(app, copies):
        total = nl_send[app, 0]
        for at, copy in enumerate(copies):
            copy.wait_recv()
            total = total + nl_recv[app, at + 1]
        own = ((lax.axis_index("gx") * 4 + lax.axis_index("gy")) * 8 + lax.axis_index("gz")) * 2
        row = lax.broadcasted_iota(jnp.int32, (2, 256), 0)
        weight = jnp.where(row == 0, coupling_ref[own], coupling_ref[own + 1])
        nl_own[app] = total * weight
        out = []
        for at, bits in enumerate(BITS):
            copy = pltpu.make_async_remote_copy(
                src_ref=nl_own.at[app],
                dst_ref=nl_back.at[app, at + 1],
                send_sem=nl_sems.at[0, app, 7 + at],
                recv_sem=nl_sems.at[1, app, 7 + at],
                device_id=neighbour(bits),
                device_id_type=MESH,
            )
            copy.start()
            out.append(copy)
        return out

    def add_nonlocal(total, app, copies):
        parts = [nl_own[app]]
        for at, copy in enumerate(copies):
            copy.wait_recv()
            parts.append(nl_back[app, at + 1])
        high, low = exact_halves(jnp.concatenate(parts, axis=0))
        back = jnp.concatenate([high, high, low], axis=0)

        def step(kx, carry):
            rows = pl.ds(block_start(kx), BLOCK)
            added = mm(proj_t[kx], back)
            for h in (0, 1):
                total[h, rows, :] = total[h, rows, :] + added[:, 128 * h : 128 * h + 128]
            return carry

        lax.fori_loop(0, 24, step, 0)

    def cells(values, total):
        total[...] = jnp.zeros((2, ROWS, 128), F32)

        def step(c, carry):
            base = (c % 2) * HALF + (c // 4) * (6 * BLOCK) + (c // 2 % 2) * 48
            rows = [pl.ds(pl.multiple_of(base + a * BLOCK, 8), 56) for a in range(7)]
            stacked = jnp.concatenate([both_halves(values, r) for r in rows], axis=0).astype(BF16)
            product = mm(pad_k[c], stacked)
            for a in range(7):
                for h in (0, 1):
                    part = product[56 * a : 56 * a + 56, 128 * h : 128 * h + 128]
                    total[h, rows[a], :] = total[h, rows[a], :] + part
            return carry

        lax.fori_loop(0, 8, step, 0)

    def join_middle(total):
        low, high = pl.ds(6, LINES, 8), pl.ds(HALF, LINES, 8)
        for h in (0, 1):
            both = total[h, low, :] + total[h, high, :]
            total[h, low, :] = both
            total[h, high, :] = both

    reduce_1 = start_coefficients(field, 0)
    all_copies += reduce_1

    col = lax.broadcasted_iota(jnp.int32, (343, PAD_NODES), 1)
    node = jnp.where((col & 7) < 7, (col >> 3) * 7 + (col & 7), -1)
    widen = jnp.where(lax.broadcasted_iota(jnp.int32, (343, PAD_NODES), 0) == node, 1.0, 0.0).astype(BF16)
    row = lax.broadcasted_iota(jnp.int32, (PAD_NODES, 343), 0)
    node = jnp.where((row & 7) < 7, (row >> 3) * 7 + (row & 7), -1)
    raise_ = jnp.where(lax.broadcasted_iota(jnp.int32, (PAD_NODES, 343), 1) == node, 1.0, 0.0).astype(BF16)

    def pad_cell(c, carry):
        wide = mm(k_ref[c], widen).astype(BF16)
        pad_k[c] = mm(raise_, wide).astype(BF16)
        return carry

    lax.fori_loop(0, 8, pad_cell, 0)

    totals_1 = start_totals(0, reduce_1)
    all_copies += totals_1
    end_exchange(field, DOWN, first, groups[0][1], False)
    cells(field, image)
    add_nonlocal(image, 0, totals_1)
    join_middle(image)
    middle = start_exchange(image, ALL, *groups[1])
    all_copies += middle
    end_exchange(image, ALL, middle, groups[1][1], True)

    reduce_2 = start_coefficients(image, 1)
    all_copies += reduce_2
    cells(image, field)
    join_middle(field)
    last = start_exchange(field, UP, *groups[2])
    all_copies += last
    totals_2 = start_totals(1, reduce_2)
    all_copies += totals_2
    add_nonlocal(field, 1, totals_2)
    end_exchange(field, UP, last, groups[2][1], True)

    def finish(x, carry):
        base = pl.multiple_of(x * BLOCK, 8)
        low = both_halves(field, pl.ds(base, 96)).reshape(12, 8, 256)
        high = pltpu.roll(both_halves(field, pl.ds(base + HALF, 96)).reshape(12, 8, 256), 6, 1)
        row = lax.broadcasted_iota(jnp.int32, (12, 8, 256), 1)
        out_ref[x, :, 0:8, :] = 2.0 * jnp.where(row < 7, low, high) - w_ref[x, :, 0:8, :]
        out_ref[x, :, 8:12, :] = 2.0 * high[:, 0:4] - w_ref[x, :, 8:12, :]
        return carry

    lax.fori_loop(0, 12, finish, 0)
    for copy in all_copies:
        copy.wait_send()


def local(wavefunctions, cell_matrices, projectors, slot_atoms, atom_coupling):
    buffers = []
    for deltas in (DOWN, ALL, UP):
        one = [
            pltpu.VMEM((2, message_rows(kind_of(d)), 128), message_type(kind_of(d))) for d in deltas
        ]
        buffers += one + one
    count = len(DOWN) + len(ALL) + len(UP)
    vmem = pl.BlockSpec(memory_space=pltpu.VMEM)
    return pl.pallas_call(
        kernel,
        out_shape=jax.ShapeDtypeStruct(wavefunctions.shape, F32),
        in_specs=[vmem, vmem, vmem, vmem, pl.BlockSpec(memory_space=pltpu.SMEM)],
        out_specs=vmem,
        scratch_shapes=[
            pltpu.VMEM((2, ROWS, 128), F32),
            pltpu.VMEM((2, ROWS, 128), F32),
            pltpu.VMEM((8, PAD_NODES, PAD_NODES), BF16),
            pltpu.VMEM((48, 1920), BF16),
            pltpu.VMEM((24, 32, BLOCK), BF16),
            pltpu.VMEM((24, BLOCK, 48), BF16),
            pltpu.VMEM((2, 8, 2, 256), F32),
            pltpu.VMEM((2, 8, 2, 256), F32),
            pltpu.VMEM((2, 2, 256), F32),
            pltpu.VMEM((2, 8, 2, 256), F32),
            pltpu.SemaphoreType.DMA((2, 2, 14)),
            pltpu.SemaphoreType.DMA((2, count)),
            *buffers,
        ],
        compiler_params=pltpu.CompilerParams(collective_id=0, has_side_effects=True, vmem_limit_bytes=60 * 1024 * 1024),
    )(
        wavefunctions,
        cell_matrices.reshape(8, 343, 343),
        projectors[0],
        slot_atoms,
        atom_coupling,
    )


def solution(mesh):
    return jax.shard_map(
        local,
        mesh=mesh,
        in_specs=(
            P("gx", "gy", "gz", None),
            P("gx", "gy", "gz", None, None),
            P(("gx", "gy", "gz"), None, None),
            P(("gx", "gy", "gz"), None),
            P(),
        ),
        out_specs=P("gx", "gy", "gz", None),
        check_vma=False,
    )
```

profile of v0, /device:TPU:1, one launch (start us, length us, event | category | flops | bytes accessed | tf_op | source)
XLA Modules:
  0.0 86.2 jit_solution(17903690272065898315)
XLA Ops:
  0.0 3.2 %copy.6 = bf16[2,2,2,343,343]{4,3,2,1,0:T(8,128)(2,1)} copy(bf16[2,2,2,343,343]{4,2,3,1,0:T(2,128)(2,1)} %param.6) | data formatting | bytes 3764768 | tf_op args[1]
  3.2 79.7 %shard_map.55 = f32[12,12,12,256]{3,2,1,0:T(8,128)} custom-call(f32[12,12,12,256]{3,2,1,0:T(8,128)} %w_ref.1, bf16[8,343,343]{2,1,0:T(8,128)(2,1)} %bitcast.2, f32[16,1728]{1,0:T(8,128)} %bitcast.3, s32[1,16]{1,0:T(1,128)} %slots_ref.1, f32[512]{0:T(512)} %coupling_ref.1), custom_call_target="tpu_custom_call" | custom-call | tf_op jit(solution)/shard_map/pallas_call | solution.py:371
  82.9 3.3 %copy.8 = f32[12,12,12,256]{3,2,1,0:T(8,128)} copy(f32[12,12,12,256]{3,2,1,0:T(8,128)} %shard_map.55) | data formatting | bytes 3538944
where the time goes:
time: 86.3 us; the launch traced here: 86.2 us
  Pallas kernels  79.7 us (92%)
  local copies, waits for them, and re-layouts  6.46 us (7%)
    pallas_call x1, Pallas kernels, local(): pl.pallas_call(kernel, out_shape=jax.ShapeDtypeStruct(wavefunctions.shape...  79.7 us
    unnamed x2, local copies, waits for them, and re-layouts  6.46 us

commit v1 on v0

--- a/solution.py
+++ b/solution.py
@@ -15,6 +15,7 @@
 HALF = LINES * 8
 ROWS = 2 * HALF
 BLOCK = 104
+PAIR = 2 * BLOCK
 PAD_NODES = 392
 
 ALL = [d for d in itertools.product((-1, 0, 1), repeat=3) if any(d)]
@@ -95,32 +96,43 @@
     return tuple(out)
 
 
-def start_exchange(field, deltas, send, recv, send_sem, recv_sem):
-    copies = []
-    for at, delta in enumerate(deltas):
-        kind = kind_of(delta)
-        coords = tuple(12 if d > 0 else 0 for d in delta)
+def exchange_copy(at, deltas, send, recv, send_sem, recv_sem):
+    return pltpu.make_async_remote_copy(
+        src_ref=send[at],
+        dst_ref=recv[at],
+        send_sem=send_sem.at[at],
+        recv_sem=recv_sem.at[at],
+        device_id=neighbour(deltas[at]),
+        device_id_type=MESH,
+    )
+
+
+def pack_message(field, at, deltas, send):
+    kind = kind_of(deltas[at])
+    coords = tuple(12 if d > 0 else 0 for d in deltas[at])
+    for h in (0, 1):
+        send[at][h] = packed(field, h, kind, coords).astype(message_type(kind))
+
+
+def start_exchange(field, chosen, deltas, group):
+    copies = {}
+    for at in chosen:
+        pack_message(field, at, deltas, group[0])
+        copies[at] = exchange_copy(at, deltas, *group)
+        copies[at].start()
+    return copies
+
+
+def end_exchange(field, deltas, copies, recv, adding):
+    for at, copy in copies.items():
+        copy.wait_recv()
+        coords = tuple(12 if d < 0 else 0 for d in deltas[at])
         for h in (0, 1):
-            send[at][h] = packed(field, h, kind, coords).astype(message_type(kind))
-        copy = pltpu.make_async_remote_copy(
-            src_ref=send[at],
-            dst_ref=recv[at],
-            send_sem=send_sem.at[at],
-            recv_sem=recv_sem.at[at],
-            device_id=neighbour(delta),
-            device_id_type=MESH,
-        )
-        copy.start()
-        copies.append(copy)
-    return copies
-
-
-def end_exchange(field, deltas, copies, recv, adding):
-    for at, delta in enumerate(deltas):
-        copies[at].wait_recv()
-        coords = tuple(12 if d < 0 else 0 for d in delta)
-        for h in (0, 1):
-            merge(field, h, kind_of(delta), coords, recv[at][h].astype(F32), adding)
+            merge(field, h, kind_of(deltas[at]), coords, recv[at][h].astype(F32), adding)
+
+
+def with_z(deltas, z):
+    return [at for at, d in enumerate(deltas) if d[2] == z]
 
 
 def exact_halves(values):
@@ -162,6 +174,7 @@
         pl.semaphore_signal(barrier, inc=1, device_id=neighbour(delta), device_id_type=MESH)
 
     field[...] = jnp.zeros((2, ROWS, 128), F32)
+    image[...] = jnp.zeros((2, ROWS, 128), F32)
 
     def spread(x, carry):
         low = w_ref[x, :, 0:8, :]
@@ -177,10 +190,8 @@
         return carry
 
     lax.fori_loop(0, 12, spread, 0)
-    pl.semaphore_wait(barrier, len(ALL))
-    all_copies = []
-    first = start_exchange(field, DOWN, *groups[0])
-    all_copies += first
+    for at in range(len(DOWN)):
+        pack_message(field, at, DOWN, groups[0][0])
 
     ids = slots_ref[...]
     owner = ids >> 1
@@ -192,44 +203,49 @@
     order = jnp.broadcast_to(place, (16, 16)) == lax.broadcasted_iota(jnp.int32, (16, 16), 0)
     order = jnp.where(order, 1.0, 0.0).astype(BF16)
     p_high, p_low = exact_halves(p_ref[...])
-    proj[...] = jnp.zeros((48, 1920), BF16)
-    p_high = mm(order, p_high).astype(BF16)
-    p_low = mm(order, p_low).astype(BF16)
+    p_high = mm(order, p_high)
+    p_low = mm(order, p_low)
+    proj[:, pl.ds(1664, 256)] = jnp.zeros((48, 256), F32)
     proj[:, pl.ds(0, 1728)] = jnp.concatenate([p_high, p_low, p_high], axis=0)
 
-    def spread_projectors(x, carry):
-        begin = pl.multiple_of((x * 144) // 128 * 128, 128)
+    def picked(position, k):
+        plane = jnp.where(position >= BLOCK, 1, 0)
+        inner = position - plane * BLOCK
+        y, r = inner >> 3, inner & 7
+        live = (y < 12) & ((r < 7) if k == 0 else ((r >= 1) & (r <= 5)))
+        return jnp.where(live, 144 * plane + 12 * y + 6 * k + r, -1)
+
+    picks = []
+    for k in (0, 1):
+        target = picked(lax.broadcasted_iota(jnp.int32, (PAIR, 1), 0), k)
+        tall = lax.broadcasted_iota(jnp.int32, (PAIR, 384), 1) == target
+        target = picked(lax.broadcasted_iota(jnp.int32, (1, PAIR), 1), k)
+        wide = lax.broadcasted_iota(jnp.int32, (384, PAIR), 0) == target
+        picks.append([jnp.where(v, 1.0, 0.0).astype(BF16) for v in (tall, wide)])
+    for pair in range(6):
+        begin = 288 * pair // 128 * 128
         window = proj[:, pl.ds(begin, 384)]
-        row = lax.broadcasted_iota(jnp.int32, (2 * BLOCK, 1), 0)
-        k = jnp.where(row >= BLOCK, 1, 0)
-        inner = row - k * BLOCK
-        y = inner >> 3
-        r = inner & 7
-        live = (y < 12) & (r < 7) & ((k == 0) | ((r >= 1) & (r <= 5)))
-        target = jnp.where(live, 144 * x - begin + 12 * y + 6 * k + r, -1)
-        pick = lax.broadcasted_iota(jnp.int32, (2 * BLOCK, 384), 1) == target
-        pick = jnp.where(pick, 1.0, 0.0)
-        for half in (0, 1):
-            sel = pick[half * BLOCK : (half + 1) * BLOCK].astype(BF16)
-            proj_t[half * 12 + x] = mm_nt(sel, window).astype(BF16)
-            proj_n[half * 12 + x] = mm_nt(window[0:32], sel).astype(BF16)
-        return carry
-
-    lax.fori_loop(0, 12, spread_projectors, 0)
-
-    def block_start(kx):
-        return pl.multiple_of((kx // 12) * HALF + (kx % 12) * BLOCK, 8)
-
-    def start_coefficients(values, app):
-        def step(kx, total):
-            high, low = exact_halves(both_halves(values, pl.ds(block_start(kx), BLOCK)))
-            rows = proj_n[kx]
+        if begin != 288 * pair:
+            window = pltpu.roll(window, 384 - (288 * pair - begin), 1)
+        window = window.astype(BF16)
+        for k in (0, 1):
+            proj_t[6 * k + pair] = mm_nt(picks[k][0], window).astype(BF16)
+            proj_n[6 * k + pair] = mm(window[0:32], picks[k][1]).astype(BF16)
+
+    def pair_rows(kp):
+        return pl.ds((kp // 6) * HALF + (kp % 6) * PAIR, PAIR)
+
+    def set_coefficients(values, app):
+        total = jnp.zeros((16, 256), F32)
+        for kp in range(12):
+            high, low = exact_halves(both_halves(values, pair_rows(kp)))
+            rows = proj_n[kp]
             both = mm(rows, high)
-            return total + both[0:16] + both[16:32] + mm(rows[0:16], low)
-
-        total = lax.fori_loop(0, 24, step, jnp.zeros((16, 256), F32))
+            total = total + (both[0:16] + (both[16:32] + mm(rows[0:16], low)))
         for g in range(8):
             nl_send[app, g] = total[2 * g : 2 * g + 2]
+
+    def start_coefficients(app):
         copies = []
         for at, bits in enumerate(BITS):
             copy = pltpu.make_async_remote_copy(
@@ -267,38 +283,31 @@
             out.append(copy)
         return out
 
-    def add_nonlocal(total, app, copies):
+    def weighted_totals(app, copies):
         parts = [nl_own[app]]
         for at, copy in enumerate(copies):
             copy.wait_recv()
             parts.append(nl_back[app, at + 1])
         high, low = exact_halves(jnp.concatenate(parts, axis=0))
-        back = jnp.concatenate([high, high, low], axis=0)
-
-        def step(kx, carry):
-            rows = pl.ds(block_start(kx), BLOCK)
-            added = mm(proj_t[kx], back)
+        return jnp.concatenate([high, high, low], axis=0)
+
+    def add_nonlocal(total, back, k):
+        for kp in range(6 * k, 6 * k + 6):
+            rows = pair_rows(kp)
+            added = mm(proj_t[kp], back)
             for h in (0, 1):
                 total[h, rows, :] = total[h, rows, :] + added[:, 128 * h : 128 * h + 128]
-            return carry
-
-        lax.fori_loop(0, 24, step, 0)
-
-    def cells(values, total):
-        total[...] = jnp.zeros((2, ROWS, 128), F32)
-
-        def step(c, carry):
-            base = (c % 2) * HALF + (c // 4) * (6 * BLOCK) + (c // 2 % 2) * 48
-            rows = [pl.ds(pl.multiple_of(base + a * BLOCK, 8), 56) for a in range(7)]
+
+    def cells(values, total, k):
+        for ij in range(4):
+            base = k * HALF + (ij // 2) * (6 * BLOCK) + (ij % 2) * 48
+            rows = [pl.ds(base + a * BLOCK, 56) for a in range(7)]
             stacked = jnp.concatenate([both_halves(values, r) for r in rows], axis=0).astype(BF16)
-            product = mm(pad_k[c], stacked)
+            product = mm(pad_k[2 * ij + k], stacked)
             for a in range(7):
                 for h in (0, 1):
                     part = product[56 * a : 56 * a + 56, 128 * h : 128 * h + 128]
                     total[h, rows[a], :] = total[h, rows[a], :] + part
-            return carry
-
-        lax.fori_loop(0, 8, step, 0)
 
     def join_middle(total):
         low, high = pl.ds(6, LINES, 8), pl.ds(HALF, LINES, 8)
@@ -307,55 +316,81 @@
             total[h, low, :] = both
             total[h, high, :] = both
 
-    reduce_1 = start_coefficients(field, 0)
-    all_copies += reduce_1
+    set_coefficients(field, 0)
+
+    pl.semaphore_wait(barrier, len(ALL))
+    waits = []
+    first = {at: exchange_copy(at, DOWN, *groups[0]) for at in range(len(DOWN))}
+    for at in [*with_z(DOWN, -1), *with_z(DOWN, 0)]:
+        first[at].start()
+    waits += first.values()
+    reduce_1 = start_coefficients(0)
+    waits += reduce_1
 
     col = lax.broadcasted_iota(jnp.int32, (343, PAD_NODES), 1)
     node = jnp.where((col & 7) < 7, (col >> 3) * 7 + (col & 7), -1)
     widen = jnp.where(lax.broadcasted_iota(jnp.int32, (343, PAD_NODES), 0) == node, 1.0, 0.0).astype(BF16)
-    row = lax.broadcasted_iota(jnp.int32, (PAD_NODES, 343), 0)
-    node = jnp.where((row & 7) < 7, (row >> 3) * 7 + (row & 7), -1)
-    raise_ = jnp.where(lax.broadcasted_iota(jnp.int32, (PAD_NODES, 343), 1) == node, 1.0, 0.0).astype(BF16)
-
-    def pad_cell(c, carry):
-        wide = mm(k_ref[c], widen).astype(BF16)
-        pad_k[c] = mm(raise_, wide).astype(BF16)
+    row = lax.broadcasted_iota(jnp.int32, (PAD_NODES, 686), 0)
+    node = jnp.where((row & 7) < 7, 2 * ((row >> 3) * 7 + (row & 7)), -5)
+    col = lax.broadcasted_iota(jnp.int32, (PAD_NODES, 686), 1)
+    raise_ = [jnp.where(col == node + k, 1.0, 0.0).astype(BF16) for k in (0, 1)]
+
+    def pad_cells(ij, carry):
+        pairs = k_ref[ij].reshape(686, 343)
+        for k in (0, 1):
+            tall = mm(raise_[k], pairs).astype(BF16)
+            pad_k[2 * ij + k] = mm(tall, widen).astype(BF16)
         return carry
 
-    lax.fori_loop(0, 8, pad_cell, 0)
-
+    lax.fori_loop(0, 4, pad_cells, 0)
     totals_1 = start_totals(0, reduce_1)
-    all_copies += totals_1
+    waits += totals_1
     end_exchange(field, DOWN, first, groups[0][1], False)
-    cells(field, image)
-    add_nonlocal(image, 0, totals_1)
+
+    cells(field, image, 1)
+    middle = start_exchange(image, with_z(ALL, 1), ALL, groups[1])
+    cells(field, image, 0)
+    back = weighted_totals(0, totals_1)
+    add_nonlocal(image, back, 0)
+    middle.update(start_exchange(image, with_z(ALL, -1), ALL, groups[1]))
+    add_nonlocal(image, back, 1)
     join_middle(image)
-    middle = start_exchange(image, ALL, *groups[1])
-    all_copies += middle
+    middle.update(start_exchange(image, with_z(ALL, 0), ALL, groups[1]))
+    waits += middle.values()
+    field[...] = jnp.zeros((2, ROWS, 128), F32)
     end_exchange(image, ALL, middle, groups[1][1], True)
 
-    reduce_2 = start_coefficients(image, 1)
-    all_copies += reduce_2
-    cells(image, field)
+    set_coefficients(image, 1)
+    reduce_2 = start_coefficients(1)
+    waits += reduce_2
+    cells(image, field, 1)
+    last = start_exchange(field, with_z(UP, 1), UP, groups[2])
+    cells(image, field, 0)
     join_middle(field)
-    last = start_exchange(field, UP, *groups[2])
-    all_copies += last
+    last.update(start_exchange(field, with_z(UP, 0), UP, groups[2]))
+    waits += last.values()
     totals_2 = start_totals(1, reduce_2)
-    all_copies += totals_2
-    add_nonlocal(field, 1, totals_2)
+    waits += totals_2
     end_exchange(field, UP, last, groups[2][1], True)
-
-    def finish(x, carry):
-        base = pl.multiple_of(x * BLOCK, 8)
-        low = both_halves(field, pl.ds(base, 96)).reshape(12, 8, 256)
-        high = pltpu.roll(both_halves(field, pl.ds(base + HALF, 96)).reshape(12, 8, 256), 6, 1)
+    back = weighted_totals(1, totals_2)
+
+    def finish(pair, carry):
+        base = pl.multiple_of(pair * PAIR, 8)
+        total = []
+        for k in (0, 1):
+            total.append(both_halves(field, pl.ds(base + k * HALF, PAIR)) + mm(proj_t[6 * k + pair], back))
         row = lax.broadcasted_iota(jnp.int32, (12, 8, 256), 1)
-        out_ref[x, :, 0:8, :] = 2.0 * jnp.where(row < 7, low, high) - w_ref[x, :, 0:8, :]
-        out_ref[x, :, 8:12, :] = 2.0 * high[:, 0:4] - w_ref[x, :, 8:12, :]
+        for plane in (0, 1):
+            x = 2 * pair + plane
+            at = plane * BLOCK
+            low = total[0][at : at + 96].reshape(12, 8, 256)
+            high = pltpu.roll(total[1][at : at + 96].reshape(12, 8, 256), 6, 1)
+            out_ref[x, :, 0:8, :] = 2.0 * jnp.where(row < 7, low, high) - w_ref[x, :, 0:8, :]
+            out_ref[x, :, 8:12, :] = 2.0 * high[:, 0:4] - w_ref[x, :, 8:12, :]
         return carry
 
-    lax.fori_loop(0, 12, finish, 0)
-    for copy in all_copies:
+    lax.fori_loop(0, 6, finish, 0)
+    for copy in waits:
         copy.wait_send()
 
 
@@ -377,9 +412,9 @@
             pltpu.VMEM((2, ROWS, 128), F32),
             pltpu.VMEM((2, ROWS, 128), F32),
             pltpu.VMEM((8, PAD_NODES, PAD_NODES), BF16),
-            pltpu.VMEM((48, 1920), BF16),
-            pltpu.VMEM((24, 32, BLOCK), BF16),
-            pltpu.VMEM((24, BLOCK, 48), BF16),
+            pltpu.VMEM((48, 1920), F32),
+            pltpu.VMEM((12, 32, PAIR), BF16),
+            pltpu.VMEM((12, PAIR, 48), BF16),
             pltpu.VMEM((2, 8, 2, 256), F32),
             pltpu.VMEM((2, 8, 2, 256), F32),
             pltpu.VMEM((2, 2, 256), F32),
@@ -388,10 +423,10 @@
             pltpu.SemaphoreType.DMA((2, count)),
             *buffers,
         ],
-        compiler_params=pltpu.CompilerParams(collective_id=0, has_side_effects=True, vmem_limit_bytes=60 * 1024 * 1024),
+        compiler_params=pltpu.CompilerParams(collective_id=0, has_side_effects=True, vmem_limit_bytes=40 * 1024 * 1024),
     )(
         wavefunctions,
-        cell_matrices.reshape(8, 343, 343),
+        cell_matrices.transpose(0, 1, 3, 2, 4).reshape(4, 343, 2, 343),
         projectors[0],
         slot_atoms,
         atom_coupling,

time: 86.3 us -> 67.3 us (0.78)
  the two profiles are of different devices: /device:TPU:1 before, /device:TPU:32 now
where the time goes in v1:
time: 67.3 us; the launch traced here: 66.4 us
  Pallas kernels  59.5 us (88%)
  local copies, waits for them, and re-layouts  6.9 us (10%)
    pallas_call x1, Pallas kernels, local(): pl.pallas_call(kernel, out_shape=jax.ShapeDtypeStruct(wavefunctions.shape...  59.5 us
    unnamed x11, local copies, waits for them, and re-layouts  6.9 us

profile of v1, /device:TPU:32, one launch (start us, length us, event | category | flops | bytes accessed | tf_op | source)
XLA Modules:
  0.0 66.4 jit_solution(12363831323025525439)
XLA Ops:
  0.0 0.0 copy-start
  0.0 1.7 %copy-done = f32[12,12,12,256]{3,2,1,0:T(8,128)S(1)} copy-done((f32[12,12,12,256]{3,2,1,0:T(8,128)S(1)}, f32[12,12,12,256]{3,2,1,0:T(8,128)}, u32[]{:S(2)}) %copy-start) | copy-done | bytes 1769496
  1.7 0.0 copy-start.1
  1.7 1.6 %copy-done.1 = bf16[2,2,2,343,343]{4,2,3,1,0:T(2,128)(2,1)S(1)} copy-done((bf16[2,2,2,343,343]{4,2,3,1,0:T(2,128)(2,1)S(1)}, bf16[2,2,2,343,343]{4,2,3,1,0:T(2,128)(2,1)}, u32[]{:S(2)}) %copy-start.1) | copy-done | bytes 1882408
  3.3 0.0 copy-start.2
  3.3 0.9 %copy-done.2 = f32[1,16,1728]{2,1,0:T(8,128)S(1)} copy-done((f32[1,16,1728]{2,1,0:T(8,128)S(1)}, f32[1,16,1728]{2,1,0:T(8,128)}, u32[]{:S(2)}) %copy-start.2) | copy-done | bytes 110616
  4.2 0.0 copy-start.3
  4.2 0.7 %copy-done.3 = f32[512]{0:T(512)S(1)} copy-done((f32[512]{0:T(512)S(1)}, f32[512]{0:T(512)}, u32[]{:S(2)}) %copy-start.3) | copy-done | bytes 2072
  4.8 0.0 copy-start.4
  4.8 0.7 copy-done.4
  5.5 59.5 %shard_map.55 = f32[12,12,12,256]{3,2,1,0:T(8,128)S(1)} custom-call(f32[12,12,12,256]{3,2,1,0:T(8,128)S(1)} %copy-done, bf16[4,343,2,343]{3,2,1,0:T(2,128)(2,1)S(1)} %bitcast.4, f32[16,1728]{1,0:T(8,128)S(1)} %bitcast.5, s32[1,16]{1,0:T(1,128)S(1)} %copy-done.4, f32[512]{0:T(512)S(1)} %copy-done.3), custom_call_target="tpu_custom_call" | custom-call | tf_op jit(solution)/shard_map/pallas_call | solution.py:406
  65.0 1.4 %copy.7 = f32[12,12,12,256]{3,2,1,0:T(8,128)} copy(f32[12,12,12,256]{3,2,1,0:T(8,128)S(1)} %shard_map.55) | data formatting | bytes 3538944
Async XLA Ops:
  0.0 1.7 %copy-start = (f32[12,12,12,256]{3,2,1,0:T(8,128)S(1)}, f32[12,12,12,256]{3,2,1,0:T(8,128)}, u32[]{:S(2)}) copy-start(f32[12,12,12,256]{3,2,1,0:T(8,128)} %w_ref.1) | copy-start | bytes 5308420
  1.7 1.6 %copy-start.1 = (bf16[2,2,2,343,343]{4,2,3,1,0:T(2,128)(2,1)S(1)}, bf16[2,2,2,343,343]{4,2,3,1,0:T(2,128)(2,1)}, u32[]{:S(2)}) copy-start(bf16[2,2,2,343,343]{4,2,3,1,0:T(2,128)(2,1)} %param.6) | copy-start | bytes 5647156
  3.3 0.9 %copy-start.2 = (f32[1,16,1728]{2,1,0:T(8,128)S(1)}, f32[1,16,1728]{2,1,0:T(8,128)}, u32[]{:S(2)}) copy-start(f32[1,16,1728]{2,1,0:T(8,128)} %param.7) | copy-start | bytes 331780
  4.2 0.7 %copy-start.3 = (f32[512]{0:T(512)S(1)}, f32[512]{0:T(512)}, u32[]{:S(2)}) copy-start(f32[512]{0:T(512)} %coupling_ref.1) | copy-start | bytes 6148
  4.8 0.7 copy-start.4

commit v2 on v1

--- a/solution.py
+++ b/solution.py
@@ -29,11 +29,11 @@
     return tuple(int(d != 0) for d in delta)
 
 
-def message_rows(kind):
+def message_rows(kind, full):
     return {
         (1, 0, 0): 208,
-        (0, 1, 0): 208,
-        (0, 0, 1): 169,
+        (0, 1, 0): 208 if full else 192,
+        (0, 0, 1): LINES if full else 156,
         (1, 1, 0): 16,
         (1, 0, 1): 13,
         (0, 1, 1): 13,
@@ -49,14 +49,14 @@
     return 0 if z == 0 else HALF + 6
 
 
-def pieces_of(kind, coords):
+def pieces_of(kind, coords, full):
     x, y, z = coords
     if kind == (1, 0, 0):
         return [(k * HALF + x * BLOCK, BLOCK, 1) for k in (0, 1)]
     if kind == (0, 1, 0):
-        return [(k * HALF + (13 * i + y) * 8, 8, 1) for k in (0, 1) for i in range(13)]
+        return [(k * HALF + (13 * i + y) * 8, 8, 1) for k in (0, 1) for i in range(13 if full else 12)]
     if kind == (0, 0, 1):
-        return [(z_row(z), LINES, 8)]
+        return [(z_row(z), LINES if full else 156, 8)]
     if kind == (1, 1, 0):
         return [(k * HALF + (13 * x + y) * 8, 8, 1) for k in (0, 1)]
     if kind == (1, 0, 1):
@@ -70,14 +70,14 @@
     return pl.ds(start, count) if stride == 1 else pl.ds(start, count, stride)
 
 
-def packed(field, h, kind, coords):
-    parts = [field[h, rows_at(*p), :] for p in pieces_of(kind, coords)]
+def packed(field, h, kind, coords, full):
+    parts = [field[h, rows_at(*p), :] for p in pieces_of(kind, coords, full)]
     return parts[0] if len(parts) == 1 else jnp.concatenate(parts, axis=0)
 
 
-def merge(field, h, kind, coords, message, adding):
+def merge(field, h, kind, coords, full, message, adding):
     at = 0
-    for start, count, stride in pieces_of(kind, coords):
+    for start, count, stride in pieces_of(kind, coords, full):
         part = message[at : at + count]
         rows = rows_at(start, count, stride)
         field[h, rows, :] = field[h, rows, :] + part if adding else part
@@ -96,43 +96,42 @@
     return tuple(out)
 
 
-def exchange_copy(at, deltas, send, recv, send_sem, recv_sem):
+def exchange_copy(at, h, deltas, group):
+    send, recv, send_sem, recv_sem = group
     return pltpu.make_async_remote_copy(
-        src_ref=send[at],
-        dst_ref=recv[at],
-        send_sem=send_sem.at[at],
-        recv_sem=recv_sem.at[at],
+        src_ref=send[at].at[h],
+        dst_ref=recv[at].at[h],
+        send_sem=send_sem.at[at, h],
+        recv_sem=recv_sem.at[at, h],
         device_id=neighbour(deltas[at]),
         device_id_type=MESH,
     )
 
 
-def pack_message(field, at, deltas, send):
+def pack_message(field, at, h, deltas, send):
     kind = kind_of(deltas[at])
     coords = tuple(12 if d > 0 else 0 for d in deltas[at])
-    for h in (0, 1):
-        send[at][h] = packed(field, h, kind, coords).astype(message_type(kind))
-
-
-def start_exchange(field, chosen, deltas, group):
+    send[at][h] = packed(field, h, kind, coords, deltas is ALL).astype(message_type(kind))
+
+
+def start_exchange(field, h, chosen, deltas, group):
     copies = {}
     for at in chosen:
-        pack_message(field, at, deltas, group[0])
-        copies[at] = exchange_copy(at, deltas, *group)
+        pack_message(field, at, h, deltas, group[0])
+        copies[at] = exchange_copy(at, h, deltas, group)
         copies[at].start()
     return copies
 
 
-def end_exchange(field, deltas, copies, recv, adding):
-    for at, copy in copies.items():
-        copy.wait_recv()
+def end_exchange(field, h, chosen, deltas, copies, recv, adding):
+    for at in chosen:
+        copies[at].wait_recv()
         coords = tuple(12 if d < 0 else 0 for d in deltas[at])
-        for h in (0, 1):
-            merge(field, h, kind_of(deltas[at]), coords, recv[at][h].astype(F32), adding)
-
-
-def with_z(deltas, z):
-    return [at for at, d in enumerate(deltas) if d[2] == z]
+        merge(field, h, kind_of(deltas[at]), coords, deltas is ALL, recv[at][h].astype(F32), adding)
+
+
+def chosen_of(deltas, test):
+    return [at for at, d in enumerate(deltas) if test(d)]
 
 
 def exact_halves(values):
@@ -148,7 +147,9 @@
     return lax.dot_general(a, b, (((1,), (1,)), ((), ())), preferred_element_type=F32)
 
 
-def kernel(w_ref, k_ref, p_ref, slots_ref, coupling_ref, out_ref, *scratch):
+def kernel(w_hbm, k_hbm, p_hbm, slots_hbm, coupling_hbm, out_ref, *scratch):
+    w_ref, k_ref, p_ref, slots_ref, coupling_ref, in_sems = scratch[:6]
+    scratch = scratch[6:]
     (field, image, pad_k, proj, proj_n, proj_t) = scratch[:6]
     nl_send, nl_recv, nl_own, nl_back, nl_sems = scratch[6:11]
     sems = scratch[11]
@@ -173,8 +174,25 @@
     for delta in ALL:
         pl.semaphore_signal(barrier, inc=1, device_id=neighbour(delta), device_id_type=MESH)
 
-    field[...] = jnp.zeros((2, ROWS, 128), F32)
-    image[...] = jnp.zeros((2, ROWS, 128), F32)
+    inputs = [
+        pltpu.make_async_copy(source, target, in_sems.at[at])
+        for at, (source, target) in enumerate(
+            (
+                (w_hbm, w_ref),
+                (slots_hbm, slots_ref),
+                (p_hbm, p_ref),
+                (coupling_hbm, coupling_ref),
+                (k_hbm, k_ref),
+            )
+        )
+    ]
+    for copy in inputs:
+        copy.start()
+
+    for k in (0, 1):
+        for x in range(12):
+            field[:, pl.ds(k * HALF + (13 * x + 12) * 8, 8), :] = jnp.zeros((2, 8, 128), F32)
+    inputs[0].wait()
 
     def spread(x, carry):
         low = w_ref[x, :, 0:8, :]
@@ -190,8 +208,11 @@
         return carry
 
     lax.fori_loop(0, 12, spread, 0)
-    for at in range(len(DOWN)):
-        pack_message(field, at, DOWN, groups[0][0])
+    for h in (0, 1):
+        for at in range(len(DOWN)):
+            pack_message(field, at, h, DOWN, groups[0][0])
+    for copy in inputs[1:4]:
+        copy.wait()
 
     ids = slots_ref[...]
     owner = ids >> 1
@@ -208,18 +229,18 @@
     proj[:, pl.ds(1664, 256)] = jnp.zeros((48, 256), F32)
     proj[:, pl.ds(0, 1728)] = jnp.concatenate([p_high, p_low, p_high], axis=0)
 
-    def picked(position, k):
+    def picked(position, k, twice):
         plane = jnp.where(position >= BLOCK, 1, 0)
         inner = position - plane * BLOCK
         y, r = inner >> 3, inner & 7
-        live = (y < 12) & ((r < 7) if k == 0 else ((r >= 1) & (r <= 5)))
+        live = (y < 12) & ((r < 7) if k == 0 else ((r >= (0 if twice else 1)) & (r <= 5)))
         return jnp.where(live, 144 * plane + 12 * y + 6 * k + r, -1)
 
     picks = []
     for k in (0, 1):
-        target = picked(lax.broadcasted_iota(jnp.int32, (PAIR, 1), 0), k)
+        target = picked(lax.broadcasted_iota(jnp.int32, (PAIR, 1), 0), k, True)
         tall = lax.broadcasted_iota(jnp.int32, (PAIR, 384), 1) == target
-        target = picked(lax.broadcasted_iota(jnp.int32, (1, PAIR), 1), k)
+        target = picked(lax.broadcasted_iota(jnp.int32, (1, PAIR), 1), k, False)
         wide = lax.broadcasted_iota(jnp.int32, (384, PAIR), 0) == target
         picks.append([jnp.where(v, 1.0, 0.0).astype(BF16) for v in (tall, wide)])
     for pair in range(6):
@@ -235,15 +256,15 @@
     def pair_rows(kp):
         return pl.ds((kp // 6) * HALF + (kp % 6) * PAIR, PAIR)
 
-    def set_coefficients(values, app):
-        total = jnp.zeros((16, 256), F32)
+    def set_coefficients(values, app, h):
+        total = jnp.zeros((16, 128), F32)
         for kp in range(12):
-            high, low = exact_halves(both_halves(values, pair_rows(kp)))
+            high, low = exact_halves(values[h, pair_rows(kp), :])
             rows = proj_n[kp]
             both = mm(rows, high)
             total = total + (both[0:16] + (both[16:32] + mm(rows[0:16], low)))
         for g in range(8):
-            nl_send[app, g] = total[2 * g : 2 * g + 2]
+            nl_send[app, g, :, pl.ds(128 * h, 128)] = total[2 * g : 2 * g + 2]
 
     def start_coefficients(app):
         copies = []
@@ -291,41 +312,40 @@
         high, low = exact_halves(jnp.concatenate(parts, axis=0))
         return jnp.concatenate([high, high, low], axis=0)
 
-    def add_nonlocal(total, back, k):
-        for kp in range(6 * k, 6 * k + 6):
+    def add_nonlocal(total, h, back):
+        for kp in range(12):
             rows = pair_rows(kp)
-            added = mm(proj_t[kp], back)
-            for h in (0, 1):
-                total[h, rows, :] = total[h, rows, :] + added[:, 128 * h : 128 * h + 128]
-
-    def cells(values, total, k):
+            total[h, rows, :] = total[h, rows, :] + mm(proj_t[kp], back[:, 128 * h : 128 * h + 128])
+
+    def cells(values, total, h, k):
         for ij in range(4):
             base = k * HALF + (ij // 2) * (6 * BLOCK) + (ij % 2) * 48
             rows = [pl.ds(base + a * BLOCK, 56) for a in range(7)]
-            stacked = jnp.concatenate([both_halves(values, r) for r in rows], axis=0).astype(BF16)
+            stacked = jnp.concatenate([values[h, r, :] for r in rows], axis=0).astype(BF16)
             product = mm(pad_k[2 * ij + k], stacked)
             for a in range(7):
-                for h in (0, 1):
-                    part = product[56 * a : 56 * a + 56, 128 * h : 128 * h + 128]
-                    total[h, rows[a], :] = total[h, rows[a], :] + part
-
-    def join_middle(total):
+                total[h, rows[a], :] = total[h, rows[a], :] + product[56 * a : 56 * a + 56]
+
+    def join_middle(total, h):
         low, high = pl.ds(6, LINES, 8), pl.ds(HALF, LINES, 8)
-        for h in (0, 1):
-            both = total[h, low, :] + total[h, high, :]
-            total[h, low, :] = both
-            total[h, high, :] = both
-
-    set_coefficients(field, 0)
+        both = total[h, low, :] + total[h, high, :]
+        total[h, low, :] = both
+        total[h, high, :] = both
+
+    for h in (0, 1):
+        set_coefficients(field, 0, h)
 
     pl.semaphore_wait(barrier, len(ALL))
     waits = []
-    first = {at: exchange_copy(at, DOWN, *groups[0]) for at in range(len(DOWN))}
-    for at in [*with_z(DOWN, -1), *with_z(DOWN, 0)]:
-        first[at].start()
-    waits += first.values()
+    first = []
+    for h in (0, 1):
+        first.append({at: exchange_copy(at, h, DOWN, groups[0]) for at in range(len(DOWN))})
+        for at in [*chosen_of(DOWN, lambda d: d[2] < 0), *chosen_of(DOWN, lambda d: d[2] == 0)]:
+            first[h][at].start()
+        waits += first[h].values()
     reduce_1 = start_coefficients(0)
     waits += reduce_1
+    image[...] = jnp.zeros((2, ROWS, 128), F32)
 
     col = lax.broadcasted_iota(jnp.int32, (343, PAD_NODES), 1)
     node = jnp.where((col & 7) < 7, (col >> 3) * 7 + (col & 7), -1)
@@ -335,6 +355,8 @@
     col = lax.broadcasted_iota(jnp.int32, (PAD_NODES, 686), 1)
     raise_ = [jnp.where(col == node + k, 1.0, 0.0).astype(BF16) for k in (0, 1)]
 
+    inputs[4].wait()
+
     def pad_cells(ij, carry):
         pairs = k_ref[ij].reshape(686, 343)
         for k in (0, 1):
@@ -345,51 +367,70 @@
     lax.fori_loop(0, 4, pad_cells, 0)
     totals_1 = start_totals(0, reduce_1)
     waits += totals_1
-    end_exchange(field, DOWN, first, groups[0][1], False)
-
-    cells(field, image, 1)
-    middle = start_exchange(image, with_z(ALL, 1), ALL, groups[1])
-    cells(field, image, 0)
-    back = weighted_totals(0, totals_1)
-    add_nonlocal(image, back, 0)
-    middle.update(start_exchange(image, with_z(ALL, -1), ALL, groups[1]))
-    add_nonlocal(image, back, 1)
-    join_middle(image)
-    middle.update(start_exchange(image, with_z(ALL, 0), ALL, groups[1]))
-    waits += middle.values()
+
+    above = chosen_of(ALL, lambda d: d[2] > 0)
+    beside = chosen_of(ALL, lambda d: d[2] == 0 and max(d) > 0)
+    below = [at for at in range(len(ALL)) if at not in above and at not in beside]
+    owned = chosen_of(ALL, lambda d: min(d) >= 0)
+    other = [at for at in range(len(ALL)) if at not in owned]
+    everything = range(len(DOWN))
+    back = None
+    middle = []
+    for h in (0, 1):
+        end_exchange(field, h, everything, DOWN, first[h], groups[0][1], False)
+        cells(field, image, h, 1)
+        copies = start_exchange(image, h, above, ALL, groups[1])
+        cells(field, image, h, 0)
+        join_middle(image, h)
+        copies.update(start_exchange(image, h, beside, ALL, groups[1]))
+        if back is None:
+            back = weighted_totals(0, totals_1)
+        add_nonlocal(image, h, back)
+        copies.update(start_exchange(image, h, below, ALL, groups[1]))
+        middle.append(copies)
+        waits += copies.values()
     field[...] = jnp.zeros((2, ROWS, 128), F32)
-    end_exchange(image, ALL, middle, groups[1][1], True)
-
-    set_coefficients(image, 1)
-    reduce_2 = start_coefficients(1)
-    waits += reduce_2
-    cells(image, field, 1)
-    last = start_exchange(field, with_z(UP, 1), UP, groups[2])
-    cells(image, field, 0)
-    join_middle(field)
-    last.update(start_exchange(field, with_z(UP, 0), UP, groups[2]))
-    waits += last.values()
+
+    last = []
+    for h in (0, 1):
+        end_exchange(image, h, owned, ALL, middle[h], groups[1][1], True)
+        set_coefficients(image, 1, h)
+        if h == 1:
+            reduce_2 = start_coefficients(1)
+            waits += reduce_2
+        end_exchange(image, h, other, ALL, middle[h], groups[1][1], True)
+        cells(image, field, h, 1)
+        copies = start_exchange(field, h, chosen_of(UP, lambda d: d[2] > 0), UP, groups[2])
+        cells(image, field, h, 0)
+        join_middle(field, h)
+        copies.update(start_exchange(field, h, chosen_of(UP, lambda d: d[2] == 0), UP, groups[2]))
+        last.append(copies)
+        waits += copies.values()
     totals_2 = start_totals(1, reduce_2)
     waits += totals_2
-    end_exchange(field, UP, last, groups[2][1], True)
-    back = weighted_totals(1, totals_2)
-
-    def finish(pair, carry):
-        base = pl.multiple_of(pair * PAIR, 8)
-        total = []
-        for k in (0, 1):
-            total.append(both_halves(field, pl.ds(base + k * HALF, PAIR)) + mm(proj_t[6 * k + pair], back))
-        row = lax.broadcasted_iota(jnp.int32, (12, 8, 256), 1)
-        for plane in (0, 1):
-            x = 2 * pair + plane
-            at = plane * BLOCK
-            low = total[0][at : at + 96].reshape(12, 8, 256)
-            high = pltpu.roll(total[1][at : at + 96].reshape(12, 8, 256), 6, 1)
-            out_ref[x, :, 0:8, :] = 2.0 * jnp.where(row < 7, low, high) - w_ref[x, :, 0:8, :]
-            out_ref[x, :, 8:12, :] = 2.0 * high[:, 0:4] - w_ref[x, :, 8:12, :]
-        return carry
-
-    lax.fori_loop(0, 6, finish, 0)
+    back = None
+    for h in (0, 1):
+        end_exchange(field, h, everything, UP, last[h], groups[2][1], True)
+        if back is None:
+            back = weighted_totals(1, totals_2)
+        lanes = slice(128 * h, 128 * h + 128)
+
+        def finish(pair, carry):
+            base = pl.multiple_of(pair * PAIR, 8)
+            total = []
+            for k in (0, 1):
+                total.append(field[h, pl.ds(base + k * HALF, PAIR), :] + mm(proj_t[6 * k + pair], back[:, lanes]))
+            row = lax.broadcasted_iota(jnp.int32, (12, 8, 128), 1)
+            for plane in (0, 1):
+                x = 2 * pair + plane
+                at = plane * BLOCK
+                low = total[0][at : at + 96].reshape(12, 8, 128)
+                high = pltpu.roll(total[1][at : at + 96].reshape(12, 8, 128), 6, 1)
+                out_ref[x, :, 0:8, lanes] = 2.0 * jnp.where(row < 7, low, high) - w_ref[x, :, 0:8, lanes]
+                out_ref[x, :, 8:12, lanes] = 2.0 * high[:, 0:4] - w_ref[x, :, 8:12, lanes]
+            return carry
+
+        lax.fori_loop(0, 6, finish, 0)
     for copy in waits:
         copy.wait_send()
 
@@ -398,7 +439,8 @@
     buffers = []
     for deltas in (DOWN, ALL, UP):
         one = [
-            pltpu.VMEM((2, message_rows(kind_of(d)), 128), message_type(kind_of(d))) for d in deltas
+            pltpu.VMEM((2, message_rows(kind_of(d), deltas is ALL), 128), message_type(kind_of(d)))
+            for d in deltas
         ]
         buffers += one + one
     count = len(DOWN) + len(ALL) + len(UP)
@@ -406,9 +448,15 @@
     return pl.pallas_call(
         kernel,
         out_shape=jax.ShapeDtypeStruct(wavefunctions.shape, F32),
-        in_specs=[vmem, vmem, vmem, vmem, pl.BlockSpec(memory_space=pltpu.SMEM)],
+        in_specs=[pl.BlockSpec(memory_space=pltpu.HBM)] * 5,
         out_specs=vmem,
         scratch_shapes=[
+            pltpu.VMEM((12, 12, 12, 256), F32),
+            pltpu.VMEM((4, 343, 2, 343), BF16),
+            pltpu.VMEM((16, 1728), F32),
+            pltpu.VMEM((1, 16), jnp.int32),
+            pltpu.SMEM((512,), F32),
+            pltpu.SemaphoreType.DMA((5,)),
             pltpu.VMEM((2, ROWS, 128), F32),
             pltpu.VMEM((2, ROWS, 128), F32),
             pltpu.VMEM((8, PAD_NODES, PAD_NODES), BF16),
@@ -420,16 +468,21 @@
             pltpu.VMEM((2, 2, 256), F32),
             pltpu.VMEM((2, 8, 2, 256), F32),
             pltpu.SemaphoreType.DMA((2, 2, 14)),
-            pltpu.SemaphoreType.DMA((2, count)),
+            pltpu.SemaphoreType.DMA((2, count, 2)),
             *buffers,
         ],
         compiler_params=pltpu.CompilerParams(collective_id=0, has_side_effects=True, vmem_limit_bytes=40 * 1024 * 1024),
     )(
-        wavefunctions,
-        cell_matrices.transpose(0, 1, 3, 2, 4).reshape(4, 343, 2, 343),
-        projectors[0],
-        slot_atoms,
-        atom_coupling,
+        *(
+            pltpu.with_memory_space_constraint(array, pltpu.HBM)
+            for array in (
+                wavefunctions,
+                cell_matrices.transpose(0, 1, 3, 2, 4).reshape(4, 343, 2, 343),
+                projectors[0],
+                slot_atoms,
+                atom_coupling,
+            )
+        )
     )
 
 

time: 67.3 us -> 61.7 us (0.917)
  local copies, waits for them, and re-layouts: 6.9 us -> 1.41 us
    unnamed x11 -> x1, local copies, waits for them, and re-layouts: 6.9 us -> 1.41 us
where the time goes in v2:
time: 61.7 us; the launch traced here: 60.7 us
  Pallas kernels  59.3 us (96%)
  local copies, waits for them, and re-layouts  1.41 us (2%)
    pallas_call x1, Pallas kernels, local(): pl.pallas_call(kernel, out_shape=jax.ShapeDtypeStruct(wavefunctions.shape...  59.3 us
    unnamed x1, local copies, waits for them, and re-layouts  1.41 us

profile of v2, /device:TPU:32, one launch (start us, length us, event | category | flops | bytes accessed | tf_op | source)
XLA Modules:
  0.0 60.7 jit_solution(14961735841787034223)
XLA Ops:
  0.0 59.3 %shard_map.55 = f32[12,12,12,256]{3,2,1,0:T(8,128)S(1)} custom-call(f32[12,12,12,256]{3,2,1,0:T(8,128)} %w_hbm.1, bf16[4,343,2,343]{3,2,1,0:T(2,128)(2,1)} %bitcast.4, f32[16,1728]{1,0:T(8,128)} %bitcast.5, s32[1,16]{1,0:T(1,128)} %slots_hbm.1, f32[512]{0:T(512)} %coupling_hbm.1), custom_call_target="tpu_custom_call" | custom-call | tf_op jit(solution)/shard_map/pallas_call | solution.py:448
  59.3 1.4 %copy.7 = f32[12,12,12,256]{3,2,1,0:T(8,128)} copy(f32[12,12,12,256]{3,2,1,0:T(8,128)S(1)} %shard_map.55) | data formatting | bytes 3538944

commit v3 on v2

--- a/solution.py
+++ b/solution.py
@@ -39,6 +39,10 @@
         (0, 1, 1): 13,
         (1, 1, 1): 1,
     }[kind]
+
+
+def tiled(rows):
+    return -(-rows // 16) * 16 if rows > 1 else 1
 
 
 def message_type(kind):
@@ -111,7 +115,8 @@
 def pack_message(field, at, h, deltas, send):
     kind = kind_of(deltas[at])
     coords = tuple(12 if d > 0 else 0 for d in deltas[at])
-    send[at][h] = packed(field, h, kind, coords, deltas is ALL).astype(message_type(kind))
+    value = packed(field, h, kind, coords, deltas is ALL).astype(message_type(kind))
+    send[at][h, pl.ds(0, value.shape[0]), :] = value
 
 
 def start_exchange(field, h, chosen, deltas, group):
@@ -127,7 +132,9 @@
     for at in chosen:
         copies[at].wait_recv()
         coords = tuple(12 if d < 0 else 0 for d in deltas[at])
-        merge(field, h, kind_of(deltas[at]), coords, deltas is ALL, recv[at][h].astype(F32), adding)
+        full = deltas is ALL
+        message = recv[at][h, pl.ds(0, message_rows(kind_of(deltas[at]), full)), :].astype(F32)
+        merge(field, h, kind_of(deltas[at]), coords, full, message, adding)
 
 
 def chosen_of(deltas, test):
@@ -151,6 +158,7 @@
     w_ref, k_ref, p_ref, slots_ref, coupling_ref, in_sems = scratch[:6]
     scratch = scratch[6:]
     (field, image, pad_k, proj, proj_n, proj_t) = scratch[:6]
+    loose, scratch = scratch[-1], scratch[:-1]
     nl_send, nl_recv, nl_own, nl_back, nl_sems = scratch[6:11]
     sems = scratch[11]
     buffers = scratch[12:]
@@ -170,10 +178,6 @@
         at += 2 * n
         sem_at += n
 
-    barrier = pltpu.get_barrier_semaphore()
-    for delta in ALL:
-        pl.semaphore_signal(barrier, inc=1, device_id=neighbour(delta), device_id_type=MESH)
-
     inputs = [
         pltpu.make_async_copy(source, target, in_sems.at[at])
         for at, (source, target) in enumerate(
@@ -188,6 +192,10 @@
     ]
     for copy in inputs:
         copy.start()
+
+    barrier = pltpu.get_barrier_semaphore()
+    for delta in ALL:
+        pl.semaphore_signal(barrier, inc=1, device_id=neighbour(delta), device_id_type=MESH)
 
     for k in (0, 1):
         for x in range(12):
@@ -319,12 +327,19 @@
 
     def cells(values, total, h, k):
         for ij in range(4):
-            base = k * HALF + (ij // 2) * (6 * BLOCK) + (ij % 2) * 48
+            i, j = ij // 2, ij % 2
+            base = k * HALF + i * (6 * BLOCK) + j * 48
             rows = [pl.ds(base + a * BLOCK, 56) for a in range(7)]
             stacked = jnp.concatenate([values[h, r, :] for r in rows], axis=0).astype(BF16)
             product = mm(pad_k[2 * ij + k], stacked)
             for a in range(7):
-                total[h, rows[a], :] = total[h, rows[a], :] + product[56 * a : 56 * a + 56]
+                shared = 56 if i and a == 0 else 8 if j else 0
+                if shared:
+                    rows = pl.ds(base + a * BLOCK, shared)
+                    total[h, rows, :] = total[h, rows, :] + product[56 * a : 56 * a + shared]
+                if shared < 56:
+                    rows = pl.ds(base + a * BLOCK + shared, 56 - shared)
+                    total[h, rows, :] = product[56 * a + shared : 56 * a + 56]
 
     def join_middle(total, h):
         low, high = pl.ds(6, LINES, 8), pl.ds(HALF, LINES, 8)
@@ -336,37 +351,39 @@
         set_coefficients(field, 0, h)
 
     pl.semaphore_wait(barrier, len(ALL))
-    waits = []
+    reduce_1 = start_coefficients(0)
+    waits = [*reduce_1]
     first = []
     for h in (0, 1):
         first.append({at: exchange_copy(at, h, DOWN, groups[0]) for at in range(len(DOWN))})
         for at in [*chosen_of(DOWN, lambda d: d[2] < 0), *chosen_of(DOWN, lambda d: d[2] == 0)]:
             first[h][at].start()
         waits += first[h].values()
-    reduce_1 = start_coefficients(0)
-    waits += reduce_1
-    image[...] = jnp.zeros((2, ROWS, 128), F32)
 
     col = lax.broadcasted_iota(jnp.int32, (343, PAD_NODES), 1)
     node = jnp.where((col & 7) < 7, (col >> 3) * 7 + (col & 7), -1)
     widen = jnp.where(lax.broadcasted_iota(jnp.int32, (343, PAD_NODES), 0) == node, 1.0, 0.0).astype(BF16)
-    row = lax.broadcasted_iota(jnp.int32, (PAD_NODES, 686), 0)
-    node = jnp.where((row & 7) < 7, 2 * ((row >> 3) * 7 + (row & 7)), -5)
-    col = lax.broadcasted_iota(jnp.int32, (PAD_NODES, 686), 1)
-    raise_ = [jnp.where(col == node + k, 1.0, 0.0).astype(BF16) for k in (0, 1)]
-
     inputs[4].wait()
 
+    loose[:, pl.ds(680, 24), :] = jnp.zeros((4, 24, 128), F32)
+
     def pad_cells(ij, carry):
-        pairs = k_ref[ij].reshape(686, 343)
-        for k in (0, 1):
-            tall = mm(raise_[k], pairs).astype(BF16)
-            pad_k[2 * ij + k] = mm(tall, widen).astype(BF16)
+        wide = mm(k_ref[ij].reshape(686, 343), widen)
+        for t in range(4):
+            width = min(128, PAD_NODES - 128 * t)
+            loose[t, pl.ds(0, 686), pl.ds(0, width)] = wide[:, 128 * t : 128 * t + width]
+        for t in range(4):
+            width = min(128, PAD_NODES - 128 * t)
+            for k in (0, 1):
+                runs = [loose[t, pl.ds(14 * run + k, 8, 2), :] for run in range(49)]
+                tall = jnp.concatenate(runs, axis=0).astype(BF16)
+                pad_k[2 * ij + k, :, pl.ds(128 * t, width)] = tall[:, 0:width]
         return carry
 
-    lax.fori_loop(0, 4, pad_cells, 0)
+    lax.fori_loop(0, 3, pad_cells, 0)
     totals_1 = start_totals(0, reduce_1)
     waits += totals_1
+    lax.fori_loop(3, 4, pad_cells, 0)
 
     above = chosen_of(ALL, lambda d: d[2] > 0)
     beside = chosen_of(ALL, lambda d: d[2] == 0 and max(d) > 0)
@@ -374,7 +391,6 @@
     owned = chosen_of(ALL, lambda d: min(d) >= 0)
     other = [at for at in range(len(ALL)) if at not in owned]
     everything = range(len(DOWN))
-    back = None
     middle = []
     for h in (0, 1):
         end_exchange(field, h, everything, DOWN, first[h], groups[0][1], False)
@@ -383,13 +399,12 @@
         cells(field, image, h, 0)
         join_middle(image, h)
         copies.update(start_exchange(image, h, beside, ALL, groups[1]))
-        if back is None:
-            back = weighted_totals(0, totals_1)
+        middle.append(copies)
+    back = weighted_totals(0, totals_1)
+    for h in (0, 1):
         add_nonlocal(image, h, back)
-        copies.update(start_exchange(image, h, below, ALL, groups[1]))
-        middle.append(copies)
-        waits += copies.values()
-    field[...] = jnp.zeros((2, ROWS, 128), F32)
+        middle[h].update(start_exchange(image, h, below, ALL, groups[1]))
+        waits += middle[h].values()
 
     last = []
     for h in (0, 1):
@@ -401,13 +416,14 @@
         end_exchange(image, h, other, ALL, middle[h], groups[1][1], True)
         cells(image, field, h, 1)
         copies = start_exchange(field, h, chosen_of(UP, lambda d: d[2] > 0), UP, groups[2])
+        if h == 1:
+            totals_2 = start_totals(1, reduce_2)
+            waits += totals_2
         cells(image, field, h, 0)
         join_middle(field, h)
         copies.update(start_exchange(field, h, chosen_of(UP, lambda d: d[2] == 0), UP, groups[2]))
         last.append(copies)
         waits += copies.values()
-    totals_2 = start_totals(1, reduce_2)
-    waits += totals_2
     back = None
     for h in (0, 1):
         end_exchange(field, h, everything, UP, last[h], groups[2][1], True)
@@ -439,7 +455,7 @@
     buffers = []
     for deltas in (DOWN, ALL, UP):
         one = [
-            pltpu.VMEM((2, message_rows(kind_of(d), deltas is ALL), 128), message_type(kind_of(d)))
+            pltpu.VMEM((2, tiled(message_rows(kind_of(d), deltas is ALL)), 128), message_type(kind_of(d)))
             for d in deltas
         ]
         buffers += one + one
@@ -470,6 +486,7 @@
             pltpu.SemaphoreType.DMA((2, 2, 14)),
             pltpu.SemaphoreType.DMA((2, count, 2)),
             *buffers,
+            pltpu.VMEM((4, 704, 128), F32),
         ],
         compiler_params=pltpu.CompilerParams(collective_id=0, has_side_effects=True, vmem_limit_bytes=40 * 1024 * 1024),
     )(

time: 61.7 us -> 60.1 us (0.974)
  the two profiles are of different devices: /device:TPU:32 before, /device:TPU:6 now
where the time goes in v3:
time: 60.1 us; the launch traced here: 60 us
  Pallas kernels  58.6 us (98%)
  local copies, waits for them, and re-layouts  1.41 us (2%)
    pallas_call x1, Pallas kernels, local(): pl.pallas_call(kernel, out_shape=jax.ShapeDtypeStruct(wavefunctions.shape...  58.6 us
    unnamed x1, local copies, waits for them, and re-layouts  1.41 us

profile of v3, /device:TPU:6, one launch (start us, length us, event | category | flops | bytes accessed | tf_op | source)
XLA Modules:
  0.0 60.0 jit_solution(601349100952121690)
XLA Ops:
  0.0 58.6 %shard_map.55 = f32[12,12,12,256]{3,2,1,0:T(8,128)S(1)} custom-call(f32[12,12,12,256]{3,2,1,0:T(8,128)} %w_hbm.1, bf16[4,343,2,343]{3,2,1,0:T(2,128)(2,1)} %bitcast.4, f32[16,1728]{1,0:T(8,128)} %bitcast.5, s32[1,16]{1,0:T(1,128)} %slots_hbm.1, f32[512]{0:T(512)} %coupling_hbm.1), custom_call_target="tpu_custom_call" | custom-call | tf_op jit(solution)/shard_map/pallas_call | solution.py:464
  58.6 1.4 %copy.7 = f32[12,12,12,256]{3,2,1,0:T(8,128)} copy(f32[12,12,12,256]{3,2,1,0:T(8,128)S(1)} %shard_map.55) | data formatting | bytes 3538944

commit v4 on v3

--- a/solution.py
+++ b/solution.py
@@ -19,7 +19,7 @@
 PAD_NODES = 392
 
 ALL = [d for d in itertools.product((-1, 0, 1), repeat=3) if any(d)]
-ALL.sort(key=lambda d: sum(map(abs, d)))
+ALL.sort(key=lambda d: (sum(map(abs, d)), -abs(d[2])))
 DOWN = [d for d in ALL if max(d) <= 0]
 UP = [d for d in ALL if min(d) >= 0]
 BITS = [d for d in itertools.product((0, 1), repeat=3) if any(d)]
@@ -32,7 +32,7 @@
 def message_rows(kind, full):
     return {
         (1, 0, 0): 208,
-        (0, 1, 0): 208 if full else 192,
+        (0, 1, 0): LINES if full else 156,
         (0, 0, 1): LINES if full else 156,
         (1, 1, 0): 16,
         (1, 0, 1): 13,
@@ -58,7 +58,8 @@
     if kind == (1, 0, 0):
         return [(k * HALF + x * BLOCK, BLOCK, 1) for k in (0, 1)]
     if kind == (0, 1, 0):
-        return [(k * HALF + (13 * i + y) * 8, 8, 1) for k in (0, 1) for i in range(13 if full else 12)]
+        nodes = [*range(7), *range(HALF + 1, HALF + 7)]
+        return [(row + y * 8, 13 if full else 12, BLOCK) for row in nodes]
     if kind == (0, 0, 1):
         return [(z_row(z), LINES if full else 156, 8)]
     if kind == (1, 1, 0):
@@ -84,7 +85,10 @@
     for start, count, stride in pieces_of(kind, coords, full):
         part = message[at : at + count]
         rows = rows_at(start, count, stride)
-        field[h, rows, :] = field[h, rows, :] + part if adding else part
+        value = field[h, rows, :] + part if adding else part
+        field[h, rows, :] = value
+        if kind == (0, 1, 0) and start == 6 + 8 * coords[1]:
+            field[h, rows_at(start - 6 + HALF, count, stride), :] = value
         at += count
 
 
@@ -129,7 +133,7 @@
 
 
 def end_exchange(field, h, chosen, deltas, copies, recv, adding):
-    for at in chosen:
+    for at in sorted(chosen, key=lambda at: abs(deltas[at][2])):
         copies[at].wait_recv()
         coords = tuple(12 if d < 0 else 0 for d in deltas[at])
         full = deltas is ALL
@@ -194,7 +198,7 @@
         copy.start()
 
     barrier = pltpu.get_barrier_semaphore()
-    for delta in ALL:
+    for delta in reversed(ALL):
         pl.semaphore_signal(barrier, inc=1, device_id=neighbour(delta), device_id_type=MESH)
 
     for k in (0, 1):
@@ -393,10 +397,12 @@
     everything = range(len(DOWN))
     middle = []
     for h in (0, 1):
-        end_exchange(field, h, everything, DOWN, first[h], groups[0][1], False)
+        end_exchange(field, h, chosen_of(DOWN, lambda d: d[2] == 0), DOWN, first[h], groups[0][1], False)
+        cells(field, image, h, 0)
+    for h in (0, 1):
+        end_exchange(field, h, chosen_of(DOWN, lambda d: d[2] < 0), DOWN, first[h], groups[0][1], False)
         cells(field, image, h, 1)
         copies = start_exchange(image, h, above, ALL, groups[1])
-        cells(field, image, h, 0)
         join_middle(image, h)
         copies.update(start_exchange(image, h, beside, ALL, groups[1]))
         middle.append(copies)
@@ -413,15 +419,16 @@
         if h == 1:
             reduce_2 = start_coefficients(1)
             waits += reduce_2
-        end_exchange(image, h, other, ALL, middle[h], groups[1][1], True)
+        end_exchange(image, h, [at for at in other if ALL[at][2] >= 0], ALL, middle[h], groups[1][1], True)
+        cells(image, field, h, 0)
+        end_exchange(image, h, [at for at in other if ALL[at][2] < 0], ALL, middle[h], groups[1][1], True)
         cells(image, field, h, 1)
         copies = start_exchange(field, h, chosen_of(UP, lambda d: d[2] > 0), UP, groups[2])
+        join_middle(field, h)
+        copies.update(start_exchange(field, h, chosen_of(UP, lambda d: d[2] == 0), UP, groups[2]))
         if h == 1:
             totals_2 = start_totals(1, reduce_2)
             waits += totals_2
-        cells(image, field, h, 0)
-        join_middle(field, h)
-        copies.update(start_exchange(field, h, chosen_of(UP, lambda d: d[2] == 0), UP, groups[2]))
         last.append(copies)
         waits += copies.values()
     back = None

time: 60.1 us -> 59.7 us (level)
  the two profiles are of different devices: /device:TPU:6 before, /device:TPU:38 now
where the time goes in v4:
time: 59.7 us; the launch traced here: 59.6 us
  Pallas kernels  58.2 us (97%)
  local copies, waits for them, and re-layouts  1.41 us (2%)
    pallas_call x1, Pallas kernels, local(): pl.pallas_call(kernel, out_shape=jax.ShapeDtypeStruct(wavefunctions.shape...  58.2 us
    unnamed x1, local copies, waits for them, and re-layouts  1.41 us

profile of v4, /device:TPU:38, one launch (start us, length us, event | category | flops | bytes accessed | tf_op | source)
XLA Modules:
  0.0 59.6 jit_solution(1369348614182331747)
XLA Ops:
  0.0 58.2 %shard_map.55 = f32[12,12,12,256]{3,2,1,0:T(8,128)S(1)} custom-call(f32[12,12,12,256]{3,2,1,0:T(8,128)} %w_hbm.1, bf16[4,343,2,343]{3,2,1,0:T(2,128)(2,1)} %bitcast.4, f32[16,1728]{1,0:T(8,128)} %bitcast.5, s32[1,16]{1,0:T(1,128)} %slots_hbm.1, f32[512]{0:T(512)} %coupling_hbm.1), custom_call_target="tpu_custom_call" | custom-call | tf_op jit(solution)/shard_map/pallas_call | solution.py:471
  58.2 1.4 %copy.7 = f32[12,12,12,256]{3,2,1,0:T(8,128)} copy(f32[12,12,12,256]{3,2,1,0:T(8,128)S(1)} %shard_map.55) | data formatting | bytes 3538944

commit v5 on v4

--- a/solution.py
+++ b/solution.py
@@ -416,9 +416,9 @@
     for h in (0, 1):
         end_exchange(image, h, owned, ALL, middle[h], groups[1][1], True)
         set_coefficients(image, 1, h)
-        if h == 1:
-            reduce_2 = start_coefficients(1)
-            waits += reduce_2
+    reduce_2 = start_coefficients(1)
+    waits += reduce_2
+    for h in (0, 1):
         end_exchange(image, h, [at for at in other if ALL[at][2] >= 0], ALL, middle[h], groups[1][1], True)
         cells(image, field, h, 0)
         end_exchange(image, h, [at for at in other if ALL[at][2] < 0], ALL, middle[h], groups[1][1], True)
@@ -426,7 +426,7 @@
         copies = start_exchange(field, h, chosen_of(UP, lambda d: d[2] > 0), UP, groups[2])
         join_middle(field, h)
         copies.update(start_exchange(field, h, chosen_of(UP, lambda d: d[2] == 0), UP, groups[2]))
-        if h == 1:
+        if h == 0:
             totals_2 = start_totals(1, reduce_2)
             waits += totals_2
         last.append(copies)

time: 59.7 us -> 56.2 us (0.941)
  the two profiles are of different devices: /device:TPU:38 before, /device:TPU:32 now
where the time goes in v5:
time: 56.2 us; the launch traced here: 56.1 us
  Pallas kernels  54.7 us (97%)
  local copies, waits for them, and re-layouts  1.41 us (3%)
    pallas_call x1, Pallas kernels, local(): pl.pallas_call(kernel, out_shape=jax.ShapeDtypeStruct(wavefunctions.shape...  54.7 us
    unnamed x1, local copies, waits for them, and re-layouts  1.41 us

profile of v5, /device:TPU:32, one launch (start us, length us, event | category | flops | bytes accessed | tf_op | source)
XLA Modules:
  0.0 56.1 jit_solution(18407649885220082718)
XLA Ops:
  0.0 54.7 %shard_map.55 = f32[12,12,12,256]{3,2,1,0:T(8,128)S(1)} custom-call(f32[12,12,12,256]{3,2,1,0:T(8,128)} %w_hbm.1, bf16[4,343,2,343]{3,2,1,0:T(2,128)(2,1)} %bitcast.4, f32[16,1728]{1,0:T(8,128)} %bitcast.5, s32[1,16]{1,0:T(1,128)} %slots_hbm.1, f32[512]{0:T(512)} %coupling_hbm.1), custom_call_target="tpu_custom_call" | custom-call | tf_op jit(solution)/shard_map/pallas_call | solution.py:471
  54.7 1.4 %copy.7 = f32[12,12,12,256]{3,2,1,0:T(8,128)} copy(f32[12,12,12,256]{3,2,1,0:T(8,128)S(1)} %shard_map.55) | data formatting | bytes 3538944

commit v6 on v5

--- a/solution.py
+++ b/solution.py
@@ -324,8 +324,8 @@
         high, low = exact_halves(jnp.concatenate(parts, axis=0))
         return jnp.concatenate([high, high, low], axis=0)
 
-    def add_nonlocal(total, h, back):
-        for kp in range(12):
+    def add_nonlocal(total, h, back, k):
+        for kp in range(6 * k, 6 * k + 6):
             rows = pair_rows(kp)
             total[h, rows, :] = total[h, rows, :] + mm(proj_t[kp], back[:, 128 * h : 128 * h + 128])
 
@@ -390,7 +390,7 @@
     lax.fori_loop(3, 4, pad_cells, 0)
 
     above = chosen_of(ALL, lambda d: d[2] > 0)
-    beside = chosen_of(ALL, lambda d: d[2] == 0 and max(d) > 0)
+    beside = chosen_of(ALL, lambda d: d[2] <= 0 and max(d) > 0)
     below = [at for at in range(len(ALL)) if at not in above and at not in beside]
     owned = chosen_of(ALL, lambda d: min(d) >= 0)
     other = [at for at in range(len(ALL)) if at not in owned]
@@ -408,8 +408,10 @@
         middle.append(copies)
     back = weighted_totals(0, totals_1)
     for h in (0, 1):
-        add_nonlocal(image, h, back)
-        middle[h].update(start_exchange(image, h, below, ALL, groups[1]))
+        add_nonlocal(image, h, back, 0)
+        middle[h].update(start_exchange(image, h, [at for at in below if ALL[at][2] < 0], ALL, groups[1]))
+        add_nonlocal(image, h, back, 1)
+        middle[h].update(start_exchange(image, h, [at for at in below if ALL[at][2] == 0], ALL, groups[1]))
         waits += middle[h].values()
 
     last = []
@@ -421,14 +423,14 @@
     for h in (0, 1):
         end_exchange(image, h, [at for at in other if ALL[at][2] >= 0], ALL, middle[h], groups[1][1], True)
         cells(image, field, h, 0)
+        if h == 1:
+            totals_2 = start_totals(1, reduce_2)
+            waits += totals_2
         end_exchange(image, h, [at for at in other if ALL[at][2] < 0], ALL, middle[h], groups[1][1], True)
         cells(image, field, h, 1)
         copies = start_exchange(field, h, chosen_of(UP, lambda d: d[2] > 0), UP, groups[2])
         join_middle(field, h)
         copies.update(start_exchange(field, h, chosen_of(UP, lambda d: d[2] == 0), UP, groups[2]))
-        if h == 0:
-            totals_2 = start_totals(1, reduce_2)
-            waits += totals_2
         last.append(copies)
         waits += copies.values()
     back = None

time: 56.2 us -> 56.8 us (1.011)
  Pallas kernels: 54.7 us -> 55.3 us
    pallas_call x1, Pallas kernels: 54.7 us -> 55.3 us  [local(): pl.pallas_call(kernel, out_shape=jax.ShapeDtypeStruct(wavefunctions.shape...]
where the time goes in v6:
time: 56.8 us; the launch traced here: 56.7 us
  Pallas kernels  55.3 us (97%)
  local copies, waits for them, and re-layouts  1.41 us (2%)
    pallas_call x1, Pallas kernels, local(): pl.pallas_call(kernel, out_shape=jax.ShapeDtypeStruct(wavefunctions.shape...  55.3 us
    unnamed x1, local copies, waits for them, and re-layouts  1.41 us

profile of v6, /device:TPU:32, one launch (start us, length us, event | category | flops | bytes accessed | tf_op | source)
XLA Modules:
  0.0 56.7 jit_solution(15493951968185323522)
XLA Ops:
  0.0 55.3 %shard_map.55 = f32[12,12,12,256]{3,2,1,0:T(8,128)S(1)} custom-call(f32[12,12,12,256]{3,2,1,0:T(8,128)} %w_hbm.1, bf16[4,343,2,343]{3,2,1,0:T(2,128)(2,1)} %bitcast.4, f32[16,1728]{1,0:T(8,128)} %bitcast.5, s32[1,16]{1,0:T(1,128)} %slots_hbm.1, f32[512]{0:T(512)} %coupling_hbm.1), custom_call_target="tpu_custom_call" | custom-call | tf_op jit(solution)/shard_map/pallas_call | solution.py:473
  55.3 1.4 %copy.7 = f32[12,12,12,256]{3,2,1,0:T(8,128)} copy(f32[12,12,12,256]{3,2,1,0:T(8,128)S(1)} %shard_map.55) | data formatting | bytes 3538944

commit v7 on v6

--- a/solution.py
+++ b/solution.py
@@ -423,10 +423,10 @@
     for h in (0, 1):
         end_exchange(image, h, [at for at in other if ALL[at][2] >= 0], ALL, middle[h], groups[1][1], True)
         cells(image, field, h, 0)
-        if h == 1:
+        end_exchange(image, h, [at for at in other if ALL[at][2] < 0], ALL, middle[h], groups[1][1], True)
+        if h == 0:
             totals_2 = start_totals(1, reduce_2)
             waits += totals_2
-        end_exchange(image, h, [at for at in other if ALL[at][2] < 0], ALL, middle[h], groups[1][1], True)
         cells(image, field, h, 1)
         copies = start_exchange(field, h, chosen_of(UP, lambda d: d[2] > 0), UP, groups[2])
         join_middle(field, h)

time: 56.8 us -> 58.7 us (1.033)
  Pallas kernels: 55.3 us -> 57.3 us
    pallas_call x1, Pallas kernels: 55.3 us -> 57.3 us  [local(): pl.pallas_call(kernel, out_shape=jax.ShapeDtypeStruct(wavefunctions.shape...]
where the time goes in v7:
time: 58.7 us
  Pallas kernels  57.3 us (98%)
  local copies, waits for them, and re-layouts  1.41 us (2%)
    pallas_call x1, Pallas kernels, local(): pl.pallas_call(kernel, out_shape=jax.ShapeDtypeStruct(wavefunctions.shape...  57.3 us
    unnamed x1, local copies, waits for them, and re-layouts  1.41 us

profile of v7, /device:TPU:32, one launch (start us, length us, event | category | flops | bytes accessed | tf_op | source)
XLA Modules:
  0.0 58.7 jit_solution(4061143862497288219)
XLA Ops:
  0.0 57.3 %shard_map.55 = f32[12,12,12,256]{3,2,1,0:T(8,128)S(1)} custom-call(f32[12,12,12,256]{3,2,1,0:T(8,128)} %w_hbm.1, bf16[4,343,2,343]{3,2,1,0:T(2,128)(2,1)} %bitcast.4, f32[16,1728]{1,0:T(8,128)} %bitcast.5, s32[1,16]{1,0:T(1,128)} %slots_hbm.1, f32[512]{0:T(512)} %coupling_hbm.1), custom_call_target="tpu_custom_call" | custom-call | tf_op jit(solution)/shard_map/pallas_call | solution.py:473
  57.3 1.4 %copy.7 = f32[12,12,12,256]{3,2,1,0:T(8,128)} copy(f32[12,12,12,256]{3,2,1,0:T(8,128)S(1)} %shard_map.55) | data formatting | bytes 3538944
